TPU v7x, 128 devices: a whole 4x4x4 slice. The times are simulated.
128 devices in a mesh: pb: 8 (over z_hi, x), ka: 16 (over z_lo, y, core).
Axes of the slice: x: 4, y: 4, z: 4 (z_hi: 2, z_lo: 2; z = z_hi * 2 + z_lo), core: 2. Of those that a mesh axis runs over, the one named last changes fastest.
Arguments:
- feat_first: bfloat16 [32768, 128], P(('pb', 'ka')), may hold values from -16 to 16
- feat_second: bfloat16 [32768, 128], P(('ka', 'pb')), may hold values from -18 to 18
- value_weight: bfloat16 [128, 128], replicated, may hold values from -0.5 to 0.5
- out_weight: bfloat16 [128, 128], replicated, may hold values from -0.5 to 0.5
- conv_weight: bfloat16 [3, 3, 128, 128], replicated, may hold values from -0.1875 to 0.1875
- conv_bias: bfloat16 [128], replicated, may hold values from -3 to 3
Outputs:
- refined: bfloat16 [128, 256, 128], P(('pb', 'ka'))
All inputs are finite; a program needn't handle non-finite values.
Results may differ from a plain program's by a relative error of at most 0.0055.
Values may be sent and summed in bfloat16 or wider, within the bound.
No kernel may reach another device: no remote copies, remote signals or barrier semaphores. Data moves between devices by JAX's collectives and lax.ppermute only.
A program may use at most 192 MiB of HBM per device.

v0:
```python
import jax
import jax.numpy as jnp
from jax import lax
from jax.sharding import PartitionSpec as P

WIMG = 256
floor_score = -1e30


def joined(value, axis, join):
    pieces = jax.tree.map(lambda part: lax.all_gather(part, axis), value)
    head = jax.tree.map(lambda part: part[0], pieces)
    tail = jax.tree.map(lambda part: part[1:], pieces)
    subtotal, _ = lax.scan(lambda subtotal, share: (join(subtotal, share), None), head, tail)
    return subtotal


def padded_2(block, sides, width):
    for axis, dim in sides:
        count = lax.axis_size(axis)
        forward = [(i, i + 1) for i in range(count - 1)]
        backward = [(target, source) for source, target in forward]
        low = lax.ppermute(
            lax.slice_in_dim(block, block.shape[dim] - width, None, axis=dim), axis, forward
        )
        high = lax.ppermute(lax.slice_in_dim(block, 0, width, axis=dim), axis, backward)
        block = jnp.concatenate([low, block, high], axis=dim)
    return block


def combine_parts(earlier, later):
    new_peak = jnp.maximum(earlier[0], later[0])
    early_factor = jnp.exp(earlier[0] - new_peak)
    late_factor = jnp.exp(later[0] - new_peak)
    new_mass = earlier[1] * early_factor + later[1] * late_factor
    new_weighted = earlier[2] * early_factor[:, None] + later[2] * late_factor[:, None]
    return (new_peak, new_mass, new_weighted)


def refine(padded, center, conv_weight, conv_bias):
    num_rows, num_cols, channels = center.shape
    accum_sum = jnp.zeros((num_rows * num_cols, channels), jnp.float32)
    for row_shift in range(3):
        for col_shift in range(3):
            window = padded[
                row_shift : row_shift + num_rows, col_shift : col_shift + num_cols
            ].reshape(num_rows * num_cols, channels)
            accum_sum = accum_sum + jnp.dot(
                window, conv_weight[row_shift, col_shift], preferred_element_type=jnp.float32
            )
    conv_out = accum_sum.reshape(num_rows, num_cols, channels) + conv_bias.astype(jnp.float32)
    return (center.astype(jnp.float32) + jax.nn.gelu(conv_out)).astype(jnp.bfloat16)


def local(feat_first, feat_second, value_weight, out_weight, conv_weight, conv_bias):
    own_rows, feat_width = feat_first.shape
    score_scale = feat_width ** (-0.5)
    values = jnp.dot(feat_second, value_weight, preferred_element_type=jnp.float32).astype(
        jnp.bfloat16
    )
    queries = lax.all_gather(feat_first, "ka", axis=0, tiled=True)
    total_rows = queries.shape[0]
    block_rows = min(1024, total_rows)
    num_blocks = total_rows // block_rows
    query_blocks = queries.reshape(num_blocks, block_rows, feat_width)
    start_carry = (
        jnp.full((num_blocks, block_rows), floor_score, jnp.float32),
        jnp.zeros((num_blocks, block_rows), jnp.float32),
        jnp.zeros((num_blocks, block_rows, feat_width), jnp.float32),
    )
    keys_part = lax.all_gather(feat_second, "pb", axis=0, tiled=True)
    values_part = lax.all_gather(values, "pb", axis=0, tiled=True)

    def update(members):
        query_block, old_peak, old_mass, old_weighted = members
        scores = (
            jnp.einsum("qc,kc->qk", query_block, keys_part, preferred_element_type=jnp.float32)
            * score_scale
        )
        new_peak = jnp.maximum(old_peak, jnp.max(scores, axis=1))
        expo = jnp.exp(scores - new_peak[:, None])
        decay_factor = jnp.exp(old_peak - new_peak)
        new_mass = old_mass * decay_factor + jnp.sum(expo, axis=1)
        new_weighted = old_weighted * decay_factor[:, None] + jnp.dot(
            expo.astype(jnp.bfloat16), values_part, preferred_element_type=jnp.float32
        )
        return (new_peak, new_mass, new_weighted)

    row_peak, row_mass, weighted = lax.map(update, (query_blocks,) + tuple(start_carry))
    row_peak = row_peak.reshape(total_rows)
    row_mass = row_mass.reshape(total_rows)
    weighted = weighted.reshape(total_rows, feat_width)
    own_start = lax.axis_index("ka") * own_rows
    merged = joined((row_peak, row_mass, weighted), "ka", combine_parts)
    mass_own = lax.dynamic_slice_in_dim(merged[1], own_start, own_rows, 0)
    weighted_own = lax.dynamic_slice_in_dim(merged[2], own_start, own_rows, 0)
    message = (weighted_own / mass_own[:, None]).astype(jnp.bfloat16)
    mixed_rows = (
        feat_first.astype(jnp.float32)
        + jnp.dot(message, out_weight, preferred_element_type=jnp.float32)
    ).astype(jnp.bfloat16)
    strip_rows = own_rows // WIMG
    strip_image = mixed_rows.reshape(strip_rows, WIMG, feat_width)
    tile_image = lax.all_to_all(strip_image, "ka", split_axis=1, concat_axis=0, tiled=True)
    padded = padded_2(tile_image, (("pb", 0), ("ka", 1)), 1)
    result = refine(padded, tile_image, conv_weight, conv_bias)
    refined = lax.all_to_all(result, "ka", split_axis=0, concat_axis=1, tiled=True)
    return refined


def solution(mesh):
    in_specs = (P(("pb", "ka"), None), P(("ka", "pb"), None), P(), P(), P(), P())
    out_specs = P(("pb", "ka"), None, None)
    return jax.shard_map(local, mesh=mesh, in_specs=in_specs, out_specs=out_specs, check_vma=False)
```

profile of v0, /device:TPU:7, one launch (start us, length us, event | category | flops | bytes accessed | tf_op | source)
XLA Modules:
  0.0 424.0 jit_solution(18136325351554592396)
XLA Ops:
  6.5 0.7 all-gather.5.cloned.1.call-update
  7.3 1.0 convolution_convert_fusion
  8.3 29.1 %all_gather.19 = bf16[2048,128]{1,0:T(8,128)(2,1)S(1)} all-gather(bf16[256,128]{1,0:T(8,128)(2,1)} %param.11), channel_id=1, replica_groups=mesh['pb'=8,'ka'=16] {'pb'}, dimensions={0}, use_global_device_ids=true | all-gather | bytes 589824 | tf_op jit(solution)/shard_map/all_gather | solution.py:71
  37.5 29.0 %all_gather.20 = bf16[2048,128]{1,0:T(8,128)(2,1)S(1)} all-gather(bf16[256,128]{1,0:T(8,128)(2,1)S(1)} %convolution_convert_fusion), channel_id=1, replica_groups=mesh['pb'=8,'ka'=16] {'pb'}, dimensions={0}, use_global_device_ids=true | all-gather | bytes 589824 | tf_op jit(solution)/shard_map/all_gather | solution.py:72
  66.5 28.9 %while.28 = (s32[]{:T(128)}, f32[4,1024]{1,0:T(4,128)S(1)}, f32[4,1024]{1,0:T(4,128)S(1)}, f32[4,1024,128]{2,1,0:T(8,128)}, bf16[4,1024,128]{2,1,0:T(8,128)(2,1)...) while((s32[]{:T(128)}, f32[4,1024]{1,0:T(4,128)S(1)}, ...), condition=%wide.region_3.4_spmd, body=%wide.region_0.3_spmd.sunk | while | flops 1090654208 | bytes 27063396 | solution.py:89
  66.5 2.3 multiply_reduce_fusion.2
  68.7 2.8 fusion.80
  71.6 1.9 fusion.79
  73.7 2.3 multiply_reduce_fusion.2
  76.0 2.8 fusion.80
  78.8 1.9 fusion.79
  80.9 2.3 multiply_reduce_fusion.2
  83.2 2.8 fusion.80
  86.0 1.9 fusion.79
  88.2 2.3 multiply_reduce_fusion.2
  90.4 2.8 fusion.80
  93.3 1.9 fusion.79
  95.4 33.9 %all-gather = f32[16,1,4096]{2,1,0:T(1,128)S(1)} all-gather(f32[1,1,4096]{2,1,0:T(1,128)S(1)} %reshape.97), channel_id=1, replica_groups=mesh['pb'=8,'ka'=16] {'ka'}, dimensions={0}, use_global_device_ids=true | all-gather | bytes 278528 | tf_op jit(solution)/shard_map/all_gather | solution.py:11
  129.4 17.3 %all-gather.1 = f32[16,1,4096]{2,1,0:T(1,128)S(1)} all-gather(f32[1,1,4096]{2,1,0:T(1,128)S(1)} %reshape.99), channel_id=1, replica_groups=mesh['pb'=8,'ka'=16] {'ka'}, dimensions={0}, use_global_device_ids=true | all-gather | bytes 278528 | tf_op jit(solution)/shard_map/all_gather | solution.py:11
  147.1 135.8 %all-gather.7.cloned.1.call-done = f32[16,4096,128]{2,1,0:T(8,128)} async-done(((f32[1,4096,128]{2,1,0:T(8,128)}), f32[16,4096,128]{2,1,0:T(8,128)}) %all-gather.7.cloned.1.call-update) | async-done | bytes 33554448 | tf_op jit(solution)/shard_map/all_gather | solution.py:11
  282.9 21.8 %slice.127 = f32[15,4096,128]{2,1,0:T(8,128)} slice(f32[16,4096,128]{2,1,0:T(8,128)} %all-gather.7.cloned.1.call-done), slice={[1:16], [0:4096], [0:128]} | slice | bytes 62914560 | tf_op jit(solution)/shard_map/slice | solution.py:13
  304.6 1.7 slice_bitcast_fusion
  306.4 63.9 %while.29 = (s32[]{:T(128)}, f32[4096]{0:T(1024)S(1)}, f32[4096]{0:T(1024)S(1)}, f32[4096,128]{1,0:T(8,128)S(1)}, f32[15,4096]{1,0:T(8,128)S(1)}, /*index=5*/f32...) while((s32[]{:T(128)}, f32[4096]{0:T(1024)S(1)}, f32[4096]{0:T(1024)S(1)}, f32[4096,128]{1,0:T(8,128)S(1)}, ...), condition=%wide.region_5.6_spmd, body=%wide.region_4.5_spmd.sunk | while | flops 1597442 | bytes 6520925 | solution.py:14
  306.5 4.2 fusion.81
  310.8 4.2 fusion.81
  315.0 4.2 fusion.81
  319.3 4.2 fusion.81
  323.6 4.2 fusion.81
  327.8 4.2 fusion.81
  332.1 4.2 fusion.81
  336.3 4.2 fusion.81
  340.6 4.2 fusion.81
  344.8 4.2 fusion.81
  349.1 4.2 fusion.81
  353.3 4.2 fusion.81
  357.6 4.2 fusion.81
  361.9 4.2 fusion.81
  366.1 4.2 fusion.81
  371.3 1.0 reduce
  372.3 9.9 %all_to_all.24 = bf16[16,2,1024]{2,1,0:T(2,128)(2,1)S(1)} all-to-all(bf16[16,2,1024]{2,1,0:T(2,128)(2,1)S(1)} %reshape.109), channel_id=1, replica_groups=mesh['pb'=8,'ka'=16] {'ka'}, dimensions={0} | all-to-all | bytes 131072 | tf_op jit(solution)/shard_map/all_to_all | solution.py:104
  382.3 4.6 %collective-permute-start = (bf16[1,16,128]{2,1,0:T(8,128)(2,1)S(1)}, bf16[1,16,128]{2,1,0:T(8,128)(2,1)S(1)}, u32[]{:S(2)}, u32[]{:S(2)}) collective-permute-start(bf16[1,16,128]{2,1,0:T(8,128)(2,1)S(1)} %copy.19), channel_id=1, source_target_pairs={{0,16},{16,32},{32,48},{48,64},{64,80},{80,96},{96,112},{1,17},{17... | collective-permute-start | bytes 12296 | tf_op jit(solution)/shard_map/ppermute | solution.py:23
  386.9 1.9 collective-permute-start.1
  388.9 6.0 %collective-permute-done.1 = bf16[1,16,128]{2,1,0:T(8,128)(2,1)S(1)} collective-permute-done((bf16[1,16,128]{2,1,0:T(8,128)(2,1)S(1)}, bf16[1,16,128]{2,1,0:T(8,128)(2,1)S(1)}, u32[]{:S(2)}, u32[]{:S(2)}) %collective-permute-start.1) | collective-permute-done | bytes 4128 | tf_op jit(solution)/shard_map/ppermute | solution.py:26
  394.9 3.9 collective-permute-start.2
  398.8 1.9 collective-permute-start.3
  400.9 2.9 collective-permute-done.3
  405.2 11.3 %all_to_all.25 = bf16[16,16,128]{2,1,0:T(8,128)(2,1)S(1)} all-to-all(bf16[16,16,128]{2,1,0:T(8,128)(2,1)S(1)} %fusion.30), channel_id=1, replica_groups=mesh['pb'=8,'ka'=16] {'ka'}, dimensions={0} | all-to-all | bytes 131072 | tf_op jit(solution)/shard_map/all_to_all | solution.py:107
  416.5 0.6 copy.56
  (100 shorter events, 4.6 us)
Async XLA Ops:
  6.5 0.8 copy-start
  6.5 59.9 %all-gather.5.cloned.1.call-start = ((), (), s32[]{:S(2)}) async-start(), calls=%async_computation.2 | async-start | bytes 1114112 | tf_op jit(solution)/shard_map/all_gather | solution.py:61
  7.3 275.6 %all-gather.7.cloned.1.call-start = ((), (), s32[]{:S(2)}) async-start(), calls=%async_computation.3 | async-start | bytes 35651584 | tf_op jit(solution)/shard_map/all_gather | solution.py:11
  306.4 64.0 %copy-start.3 = (bf16[256,128]{1,0:T(8,128)(2,1)S(1)}, bf16[256,128]{1,0:T(8,128)(2,1)}, u32[]{:S(2)}) copy-start(bf16[256,128]{1,0:T(8,128)(2,1)} %param.10) | copy-start | bytes 196612
  306.4 64.0 %copy-start.4 = (bf16[128,128]{1,0:T(8,128)(2,1)S(1)}, bf16[128,128]{1,0:T(8,128)(2,1)}, u32[]{:S(2)}) copy-start(bf16[128,128]{1,0:T(8,128)(2,1)} %param.13) | copy-start | bytes 98308
  306.4 82.4 %copy-start.5 = (bf16[128]{0:T(256)(128)(2,1)S(1)}, bf16[128]{0:T(256)(128)(2,1)}, u32[]{:S(2)}) copy-start(bf16[128]{0:T(256)(128)(2,1)} %param.15) | copy-start | bytes 772
  306.4 94.3 %copy-start.2 = (bf16[3,3,128,128]{3,2,1,0:T(8,128)(2,1)S(1)}, bf16[3,3,128,128]{3,2,1,0:T(8,128)(2,1)}, u32[]{:S(2)}) copy-start(bf16[3,3,128,128]{3,2,1,0:T(8,128)(2,1)} %param.14) | copy-start | bytes 884740
  370.3 46.8 %copy-start.1 = (bf16[128,128]{1,0:T(8,128)(2,1)S(1)}, bf16[128,128]{1,0:T(8,128)(2,1)}, u32[]{:S(2)}) copy-start(bf16[128,128]{1,0:T(8,128)(2,1)} %param.12) | copy-start | bytes 98308
  382.3 6.6 %collective-permute-start = (bf16[1,16,128]{2,1,0:T(8,128)(2,1)S(1)}, bf16[1,16,128]{2,1,0:T(8,128)(2,1)S(1)}, u32[]{:S(2)}, u32[]{:S(2)}) collective-permute-start(bf16[1,16,128]{2,1,0:T(8,128)(2,1)S(1)} %copy.19), channel_id=1, source_target_pairs={{0,16},{16,32},{32,48},{48,64},{64,80},{80,96},{96,112},{1,17},{17... | collective-permute-start | bytes 12296 | tf_op jit(solution)/shard_map/ppermute | solution.py:23
  386.9 8.0 %collective-permute-start.1 = (bf16[1,16,128]{2,1,0:T(8,128)(2,1)S(1)}, bf16[1,16,128]{2,1,0:T(8,128)(2,1)S(1)}, u32[]{:S(2)}, u32[]{:S(2)}) collective-permute-start(bf16[1,16,128]{2,1,0:T(8,128)(2,1)S(1)} %copy.20), channel_id=1, source_target_pairs={{16,0},{32,16},{48,32},{64,48},{80,64},{96,80},{112,96},{17,1},{33... | collective-permute-start | bytes 12296 | tf_op jit(solution)/shard_map/ppermute | solution.py:26
  394.9 6.0 %collective-permute-start.2 = (bf16[18,1,128]{2,1,0:T(2,128)(2,1)S(1)}, bf16[18,1,128]{2,1,0:T(2,128)(2,1)S(1)}, u32[]{:S(2)}, u32[]{:S(2)}) collective-permute-start(bf16[18,1,128]{2,1,0:T(2,128)(2,1)S(1)} %get-tuple-element.135), channel_id=1, source_target_pairs={{0,1},{1,2},{2,3},{3,4},{4,5},{5,6},{6,7},{7,8},{8,9},{9,10},{10,1... | collective-permute-start | bytes 13832 | tf_op jit(solution)/shard_map/ppermute | solution.py:23
  398.8 5.0 %collective-permute-start.3 = (bf16[18,1,128]{2,1,0:T(2,128)(2,1)S(1)}, bf16[18,1,128]{2,1,0:T(2,128)(2,1)S(1)}, u32[]{:S(2)}, u32[]{:S(2)}) collective-permute-start(bf16[18,1,128]{2,1,0:T(2,128)(2,1)S(1)} %get-tuple-element.136), channel_id=1, source_target_pairs={{1,0},{2,1},{3,2},{4,3},{5,4},{6,5},{7,6},{8,7},{9,8},{10,9},{11,1... | collective-permute-start | bytes 13832 | tf_op jit(solution)/shard_map/ppermute | solution.py:26
Sparse Core Ops, SparseCore 0:
  9.0 35.1 all-gather.4
  95.5 187.3 all-gather.6
where the time goes:
time: 426 us; the launch traced here: 424 us
  waiting for transfers between devices  145 us (34%)
  blocking collectives  131 us (31%)
  other arithmetic  71.8 us (17%)
  local copies, waits for them, and re-layouts  26.5 us (6%)
  matrix products  23 us (5%)
  between operations  13.8 us (3%)
  starting transfers between devices  12.4 us (3%)
    all_gather x1, waiting for transfers between devices, joined(): pieces = jax.tree.map(lambda part: lax.all_gather(part, axis), value)  136 us
    add x15, other arithmetic, combine_parts(): earlier[2] * early_factor[:, None] + later[2] * late_factor[:, None]  62.5 us
    all_gather x2, blocking collectives, joined(): pieces = jax.tree.map(lambda part: lax.all_gather(part, axis), value)  51.2 us
    all_gather x1, blocking collectives, local(): keys_part = lax.all_gather(feat_second, 'pb', axis=0, tiled=True)  29.1 us
    all_gather x1, blocking collectives, local(): values_part = lax.all_gather(values, 'pb', axis=0, tiled=True)  29 us
    slice x3, local copies, waits for them, and re-layouts, joined(): tail = jax.tree.map(lambda part: part[1:], pieces)  21.8 us
    dot_general x4, matrix products, update(): jnp.dot(expo.astype(jnp.bfloat16), values_part, preferred_element_type=jn...  11.4 us
    all_to_all x1, blocking collectives, local(): lax.all_to_all(result, 'ka', split_axis=0, concat_axis=1, tiled=True)  11.3 us
  transfers between devices with their start and end apart: 6, of which 3 were waited for; matrix products, arithmetic and copies ran while one was open for 0% of the time, Pallas kernels for 0%

commit v1 on v0

--- a/solution.py
+++ b/solution.py
@@ -2,6 +2,7 @@
 import jax.numpy as jnp
 from jax import lax
 from jax.sharding import PartitionSpec as P
+from jax.lax import all_to_all, axis_size
 
 WIMG = 256
 floor_score = -1e30
@@ -68,7 +69,9 @@
         jnp.zeros((num_blocks, block_rows), jnp.float32),
         jnp.zeros((num_blocks, block_rows, feat_width), jnp.float32),
     )
-    keys_part = lax.all_gather(feat_second, "pb", axis=0, tiled=True)
+    keys_part = jnp.concatenate(
+        all_to_all(jnp.stack([feat_second for _ in range(axis_size("pb"))]), "pb", 0, 0), axis=0
+    )
     values_part = lax.all_gather(values, "pb", axis=0, tiled=True)
 
     def update(members):

time: 426 us -> 399 us (0.937)
  blocking collectives: 131 us -> 96.1 us
  starting transfers between devices: 12.4 us -> 19.7 us
    all_gather x1 -> x0, blocking collectives: 29.1 us -> none  [local(): keys_part = lax.all_gather(feat_second, 'pb', axis=0, tiled=True)]
    all_to_all x0 -> x1, starting transfers between devices: none -> 7.53 us  [local(): all_to_all(jnp.stack([feat_second for _ in range(axis_size('pb'))]), 'pb'...]
    all_gather x2, blocking collectives: 51.2 us -> 45.5 us  [joined(): pieces = jax.tree.map(lambda part: lax.all_gather(part, axis), value)]
  transfers between devices with their start and end apart: 6 -> 7, of which waited for: 3 -> 3; matrix products, arithmetic and copies ran while one was open for 0% -> 1% of each run, Pallas kernels for 0% -> 0%
where the time goes in v1:
time: 399 us; the launch traced here: 398 us
  waiting for transfers between devices  144 us (36%)
  blocking collectives  96.1 us (24%)
  other arithmetic  71.8 us (18%)
  local copies, waits for them, and re-layouts  28.2 us (7%)
  matrix products  23 us (6%)
  starting transfers between devices  19.7 us (5%)
  between operations  13.7 us (3%)
    all_gather x1, waiting for transfers between devices, joined(): pieces = jax.tree.map(lambda part: lax.all_gather(part, axis), value)  135 us
    add x15, other arithmetic, combine_parts(): earlier[2] * early_factor[:, None] + later[2] * late_factor[:, None]  62.5 us
    all_gather x2, blocking collectives, joined(): pieces = jax.tree.map(lambda part: lax.all_gather(part, axis), value)  45.5 us
    all_gather x1, blocking collectives, local(): values_part = lax.all_gather(values, 'pb', axis=0, tiled=True)  29.5 us
    slice x3, local copies, waits for them, and re-layouts, joined(): tail = jax.tree.map(lambda part: part[1:], pieces)  21.8 us
    dot_general x4, matrix products, update(): jnp.dot(expo.astype(jnp.bfloat16), values_part, preferred_element_type=jn...  11.4 us
    all_to_all x1, blocking collectives, local(): lax.all_to_all(result, 'ka', split_axis=0, concat_axis=1, tiled=True)  11.3 us
    all_to_all x1, blocking collectives, local(): lax.all_to_all(strip_image, 'ka', split_axis=1, concat_axis=0, tiled=True)  9.75 us
  transfers between devices with their start and end apart: 7, of which 3 were waited for; matrix products, arithmetic and copies ran while one was open for 1% of the time, Pallas kernels for 0%

profile of v1, /device:TPU:7, one launch (start us, length us, event | category | flops | bytes accessed | tf_op | source)
XLA Modules:
  0.0 397.6 jit_solution(228262811801622939)
XLA Ops:
  6.5 0.7 all-gather.5.cloned.1.call-update
  7.3 1.7 stack.2
  9.0 7.5 %all-to-all-start = ((bf16[8,256,128]{2,1,0:T(8,128)(2,1)}), bf16[8,256,128]{2,1,0:T(8,128)(2,1)S(1)}, u32[]{:S(2)}, u32[]{:S(2)}) async-start(bf16[8,256,128]{2,1,0:T(8,128)(2,1)} %stack.2), calls=%async_computation | async-start | bytes 1048576 | tf_op jit(solution)/shard_map/all_to_all | solution.py:73
  16.5 1.0 convolution_convert_fusion
  17.5 29.5 %all_gather.16 = bf16[2048,128]{1,0:T(8,128)(2,1)S(1)} all-gather(bf16[256,128]{1,0:T(8,128)(2,1)S(1)} %convolution_convert_fusion), channel_id=1, replica_groups=mesh['pb'=8,'ka'=16] {'pb'}, dimensions={0}, use_global_device_ids=true | all-gather | bytes 589824 | tf_op jit(solution)/shard_map/all_gather | solution.py:75
  47.1 28.9 %while.28 = (s32[]{:T(128)}, f32[4,1024]{1,0:T(4,128)S(1)}, f32[4,1024]{1,0:T(4,128)S(1)}, f32[4,1024,128]{2,1,0:T(8,128)}, bf16[4,1024,128]{2,1,0:T(8,128)(2,1)...) while((s32[]{:T(128)}, f32[4,1024]{1,0:T(4,128)S(1)}, ...), condition=%wide.region_3.4_spmd, body=%wide.region_0.3_spmd.sunk | while | flops 1090654208 | bytes 27063396 | solution.py:92
  47.1 2.3 multiply_reduce_fusion.2
  49.3 2.8 fusion.80
  52.2 1.9 fusion.79
  54.3 2.3 multiply_reduce_fusion.2
  56.6 2.8 fusion.80
  59.4 1.9 fusion.79
  61.5 2.3 multiply_reduce_fusion.2
  63.8 2.8 fusion.80
  66.7 1.9 fusion.79
  68.8 2.3 multiply_reduce_fusion.2
  71.1 2.8 fusion.80
  73.9 1.9 fusion.79
  76.1 28.2 %all-gather.1 = f32[16,1,4096]{2,1,0:T(1,128)S(1)} all-gather(f32[1,1,4096]{2,1,0:T(1,128)S(1)} %reshape.105), channel_id=1, replica_groups=mesh['pb'=8,'ka'=16] {'ka'}, dimensions={0}, use_global_device_ids=true | all-gather | bytes 278528 | tf_op jit(solution)/shard_map/all_gather | solution.py:12
  104.3 17.3 %all-gather = f32[16,1,4096]{2,1,0:T(1,128)S(1)} all-gather(f32[1,1,4096]{2,1,0:T(1,128)S(1)} %reshape.103), channel_id=1, replica_groups=mesh['pb'=8,'ka'=16] {'ka'}, dimensions={0}, use_global_device_ids=true | all-gather | bytes 278528 | tf_op jit(solution)/shard_map/all_gather | solution.py:12
  122.0 134.8 %all-gather.7.cloned.1.call-done = f32[16,4096,128]{2,1,0:T(8,128)} async-done(((f32[1,4096,128]{2,1,0:T(8,128)}), f32[16,4096,128]{2,1,0:T(8,128)}) %all-gather.7.cloned.1.call-update) | async-done | bytes 33554448 | tf_op jit(solution)/shard_map/all_gather | solution.py:12
  256.8 21.8 %slice.127 = f32[15,4096,128]{2,1,0:T(8,128)} slice(f32[16,4096,128]{2,1,0:T(8,128)} %all-gather.7.cloned.1.call-done), slice={[1:16], [0:4096], [0:128]} | slice | bytes 62914560 | tf_op jit(solution)/shard_map/slice | solution.py:14
  278.6 1.7 slice_bitcast_fusion
  280.4 63.9 %while.29 = (s32[]{:T(128)}, f32[4096]{0:T(1024)S(1)}, f32[4096]{0:T(1024)S(1)}, f32[4096,128]{1,0:T(8,128)S(1)}, f32[15,4096]{1,0:T(8,128)S(1)}, /*index=5*/f32...) while((s32[]{:T(128)}, f32[4096]{0:T(1024)S(1)}, f32[4096]{0:T(1024)S(1)}, f32[4096,128]{1,0:T(8,128)S(1)}, ...), condition=%wide.region_5.6_spmd, body=%wide.region_4.5_spmd.sunk | while | flops 1597442 | bytes 6520925 | solution.py:15
  280.5 4.2 %fusion.81 = f32[4096,128]{1,0:T(8,128)S(1)} fusion(f32[15,4096,128]{2,1,0:T(8,128)} %get-tuple-element.297, s32[]{:T(128)} %get-tuple-element.283, f32[4096,128]{1,0:T(8,128)S(1)} %get-tuple-element.286, f32[4096]{0:T(1024)S(1)} %get-tuple-element.246, f32[4096]{0:T(1024)S(1)} %get-tuple-element.247), kind=kLoop, calls=%fused_computation.17.clone.1 | loop fusion | flops 1572864 | bytes 6324228 | tf_op jit(solution)/shard_map/while/body/eval_jaxpr/add | solution.py:37
  284.7 4.2 %fusion.81 = f32[4096,128]{1,0:T(8,128)S(1)} fusion(f32[15,4096,128]{2,1,0:T(8,128)} %get-tuple-element.297, s32[]{:T(128)} %get-tuple-element.283, f32[4096,128]{1,0:T(8,128)S(1)} %get-tuple-element.286, f32[4096]{0:T(1024)S(1)} %get-tuple-element.246, f32[4096]{0:T(1024)S(1)} %get-tuple-element.247), kind=kLoop, calls=%fused_computation.17.clone.1 | loop fusion | flops 1572864 | bytes 6324228 | tf_op jit(solution)/shard_map/while/body/eval_jaxpr/add | solution.py:37
  289.0 4.2 %fusion.81 = f32[4096,128]{1,0:T(8,128)S(1)} fusion(f32[15,4096,128]{2,1,0:T(8,128)} %get-tuple-element.297, s32[]{:T(128)} %get-tuple-element.283, f32[4096,128]{1,0:T(8,128)S(1)} %get-tuple-element.286, f32[4096]{0:T(1024)S(1)} %get-tuple-element.246, f32[4096]{0:T(1024)S(1)} %get-tuple-element.247), kind=kLoop, calls=%fused_computation.17.clone.1 | loop fusion | flops 1572864 | bytes 6324228 | tf_op jit(solution)/shard_map/while/body/eval_jaxpr/add | solution.py:37
  293.3 4.2 %fusion.81 = f32[4096,128]{1,0:T(8,128)S(1)} fusion(f32[15,4096,128]{2,1,0:T(8,128)} %get-tuple-element.297, s32[]{:T(128)} %get-tuple-element.283, f32[4096,128]{1,0:T(8,128)S(1)} %get-tuple-element.286, f32[4096]{0:T(1024)S(1)} %get-tuple-element.246, f32[4096]{0:T(1024)S(1)} %get-tuple-element.247), kind=kLoop, calls=%fused_computation.17.clone.1 | loop fusion | flops 1572864 | bytes 6324228 | tf_op jit(solution)/shard_map/while/body/eval_jaxpr/add | solution.py:37
  297.5 4.2 %fusion.81 = f32[4096,128]{1,0:T(8,128)S(1)} fusion(f32[15,4096,128]{2,1,0:T(8,128)} %get-tuple-element.297, s32[]{:T(128)} %get-tuple-element.283, f32[4096,128]{1,0:T(8,128)S(1)} %get-tuple-element.286, f32[4096]{0:T(1024)S(1)} %get-tuple-element.246, f32[4096]{0:T(1024)S(1)} %get-tuple-element.247), kind=kLoop, calls=%fused_computation.17.clone.1 | loop fusion | flops 1572864 | bytes 6324228 | tf_op jit(solution)/shard_map/while/body/eval_jaxpr/add | solution.py:37
  301.8 4.2 %fusion.81 = f32[4096,128]{1,0:T(8,128)S(1)} fusion(f32[15,4096,128]{2,1,0:T(8,128)} %get-tuple-element.297, s32[]{:T(128)} %get-tuple-element.283, f32[4096,128]{1,0:T(8,128)S(1)} %get-tuple-element.286, f32[4096]{0:T(1024)S(1)} %get-tuple-element.246, f32[4096]{0:T(1024)S(1)} %get-tuple-element.247), kind=kLoop, calls=%fused_computation.17.clone.1 | loop fusion | flops 1572864 | bytes 6324228 | tf_op jit(solution)/shard_map/while/body/eval_jaxpr/add | solution.py:37
  306.0 4.2 %fusion.81 = f32[4096,128]{1,0:T(8,128)S(1)} fusion(f32[15,4096,128]{2,1,0:T(8,128)} %get-tuple-element.297, s32[]{:T(128)} %get-tuple-element.283, f32[4096,128]{1,0:T(8,128)S(1)} %get-tuple-element.286, f32[4096]{0:T(1024)S(1)} %get-tuple-element.246, f32[4096]{0:T(1024)S(1)} %get-tuple-element.247), kind=kLoop, calls=%fused_computation.17.clone.1 | loop fusion | flops 1572864 | bytes 6324228 | tf_op jit(solution)/shard_map/while/body/eval_jaxpr/add | solution.py:37
  310.3 4.2 %fusion.81 = f32[4096,128]{1,0:T(8,128)S(1)} fusion(f32[15,4096,128]{2,1,0:T(8,128)} %get-tuple-element.297, s32[]{:T(128)} %get-tuple-element.283, f32[4096,128]{1,0:T(8,128)S(1)} %get-tuple-element.286, f32[4096]{0:T(1024)S(1)} %get-tuple-element.246, f32[4096]{0:T(1024)S(1)} %get-tuple-element.247), kind=kLoop, calls=%fused_computation.17.clone.1 | loop fusion | flops 1572864 | bytes 6324228 | tf_op jit(solution)/shard_map/while/body/eval_jaxpr/add | solution.py:37
  314.5 4.2 %fusion.81 = f32[4096,128]{1,0:T(8,128)S(1)} fusion(f32[15,4096,128]{2,1,0:T(8,128)} %get-tuple-element.297, s32[]{:T(128)} %get-tuple-element.283, f32[4096,128]{1,0:T(8,128)S(1)} %get-tuple-element.286, f32[4096]{0:T(1024)S(1)} %get-tuple-element.246, f32[4096]{0:T(1024)S(1)} %get-tuple-element.247), kind=kLoop, calls=%fused_computation.17.clone.1 | loop fusion | flops 1572864 | bytes 6324228 | tf_op jit(solution)/shard_map/while/body/eval_jaxpr/add | solution.py:37
  318.8 4.2 %fusion.81 = f32[4096,128]{1,0:T(8,128)S(1)} fusion(f32[15,4096,128]{2,1,0:T(8,128)} %get-tuple-element.297, s32[]{:T(128)} %get-tuple-element.283, f32[4096,128]{1,0:T(8,128)S(1)} %get-tuple-element.286, f32[4096]{0:T(1024)S(1)} %get-tuple-element.246, f32[4096]{0:T(1024)S(1)} %get-tuple-element.247), kind=kLoop, calls=%fused_computation.17.clone.1 | loop fusion | flops 1572864 | bytes 6324228 | tf_op jit(solution)/shard_map/while/body/eval_jaxpr/add | solution.py:37
  323.0 4.2 %fusion.81 = f32[4096,128]{1,0:T(8,128)S(1)} fusion(f32[15,4096,128]{2,1,0:T(8,128)} %get-tuple-element.297, s32[]{:T(128)} %get-tuple-element.283, f32[4096,128]{1,0:T(8,128)S(1)} %get-tuple-element.286, f32[4096]{0:T(1024)S(1)} %get-tuple-element.246, f32[4096]{0:T(1024)S(1)} %get-tuple-element.247), kind=kLoop, calls=%fused_computation.17.clone.1 | loop fusion | flops 1572864 | bytes 6324228 | tf_op jit(solution)/shard_map/while/body/eval_jaxpr/add | solution.py:37
  327.3 4.2 %fusion.81 = f32[4096,128]{1,0:T(8,128)S(1)} fusion(f32[15,4096,128]{2,1,0:T(8,128)} %get-tuple-element.297, s32[]{:T(128)} %get-tuple-element.283, f32[4096,128]{1,0:T(8,128)S(1)} %get-tuple-element.286, f32[4096]{0:T(1024)S(1)} %get-tuple-element.246, f32[4096]{0:T(1024)S(1)} %get-tuple-element.247), kind=kLoop, calls=%fused_computation.17.clone.1 | loop fusion | flops 1572864 | bytes 6324228 | tf_op jit(solution)/shard_map/while/body/eval_jaxpr/add | solution.py:37
  331.6 4.2 %fusion.81 = f32[4096,128]{1,0:T(8,128)S(1)} fusion(f32[15,4096,128]{2,1,0:T(8,128)} %get-tuple-element.297, s32[]{:T(128)} %get-tuple-element.283, f32[4096,128]{1,0:T(8,128)S(1)} %get-tuple-element.286, f32[4096]{0:T(1024)S(1)} %get-tuple-element.246, f32[4096]{0:T(1024)S(1)} %get-tuple-element.247), kind=kLoop, calls=%fused_computation.17.clone.1 | loop fusion | flops 1572864 | bytes 6324228 | tf_op jit(solution)/shard_map/while/body/eval_jaxpr/add | solution.py:37
  335.8 4.2 %fusion.81 = f32[4096,128]{1,0:T(8,128)S(1)} fusion(f32[15,4096,128]{2,1,0:T(8,128)} %get-tuple-element.297, s32[]{:T(128)} %get-tuple-element.283, f32[4096,128]{1,0:T(8,128)S(1)} %get-tuple-element.286, f32[4096]{0:T(1024)S(1)} %get-tuple-element.246, f32[4096]{0:T(1024)S(1)} %get-tuple-element.247), kind=kLoop, calls=%fused_computation.17.clone.1 | loop fusion | flops 1572864 | bytes 6324228 | tf_op jit(solution)/shard_map/while/body/eval_jaxpr/add | solution.py:37
  340.1 4.2 %fusion.81 = f32[4096,128]{1,0:T(8,128)S(1)} fusion(f32[15,4096,128]{2,1,0:T(8,128)} %get-tuple-element.297, s32[]{:T(128)} %get-tuple-element.283, f32[4096,128]{1,0:T(8,128)S(1)} %get-tuple-element.286, f32[4096]{0:T(1024)S(1)} %get-tuple-element.246, f32[4096]{0:T(1024)S(1)} %get-tuple-element.247), kind=kLoop, calls=%fused_computation.17.clone.1 | loop fusion | flops 1572864 | bytes 6324228 | tf_op jit(solution)/shard_map/while/body/eval_jaxpr/add | solution.py:37
  345.2 1.0 reduce
  346.2 9.8 %all_to_all.29 = bf16[16,2,1024]{2,1,0:T(2,128)(2,1)S(1)} all-to-all(bf16[16,2,1024]{2,1,0:T(2,128)(2,1)S(1)} %reshape.115), channel_id=1, replica_groups=mesh['pb'=8,'ka'=16] {'ka'}, dimensions={0} | all-to-all | bytes 131072 | tf_op jit(solution)/shard_map/all_to_all | solution.py:107
  356.1 4.5 %collective-permute-start = (bf16[1,16,128]{2,1,0:T(8,128)(2,1)S(1)}, bf16[1,16,128]{2,1,0:T(8,128)(2,1)S(1)}, u32[]{:S(2)}, u32[]{:S(2)}) collective-permute-start(bf16[1,16,128]{2,1,0:T(8,128)(2,1)S(1)} %copy.19), channel_id=1, source_target_pairs={{0,16},{16,32},{32,48},{48,64},{64,80},{80,96},{96,112},{1,17},{17... | collective-permute-start | bytes 12296 | tf_op jit(solution)/shard_map/ppermute | solution.py:24
  360.6 1.9 collective-permute-start.1
  362.6 6.0 %collective-permute-done.1 = bf16[1,16,128]{2,1,0:T(8,128)(2,1)S(1)} collective-permute-done((bf16[1,16,128]{2,1,0:T(8,128)(2,1)S(1)}, bf16[1,16,128]{2,1,0:T(8,128)(2,1)S(1)}, u32[]{:S(2)}, u32[]{:S(2)}) %collective-permute-start.1) | collective-permute-done | bytes 4128 | tf_op jit(solution)/shard_map/ppermute | solution.py:27
  368.6 3.9 collective-permute-start.2
  372.5 1.9 collective-permute-start.3
  374.6 2.9 collective-permute-done.3
  378.9 11.3 %all_to_all.30 = bf16[16,16,128]{2,1,0:T(8,128)(2,1)S(1)} all-to-all(bf16[16,16,128]{2,1,0:T(8,128)(2,1)S(1)} %fusion.30), channel_id=1, replica_groups=mesh['pb'=8,'ka'=16] {'ka'}, dimensions={0} | all-to-all | bytes 131072 | tf_op jit(solution)/shard_map/all_to_all | solution.py:110
  (102 shorter events, 5.2 us)
Async XLA Ops:
  6.5 10.0 %copy-start = (bf16[128,128]{1,0:T(8,128)(2,1)S(1)}, bf16[128,128]{1,0:T(8,128)(2,1)}, u32[]{:S(2)}) copy-start(bf16[128,128]{1,0:T(8,128)(2,1)} %param.12) | copy-start | bytes 98308
  6.5 40.5 %all-gather.5.cloned.1.call-start = ((), (), s32[]{:S(2)}) async-start(), calls=%async_computation.3 | async-start | bytes 1114112 | tf_op jit(solution)/shard_map/all_gather | solution.py:62
  9.0 38.1 %all-to-all-start = ((bf16[8,256,128]{2,1,0:T(8,128)(2,1)}), bf16[8,256,128]{2,1,0:T(8,128)(2,1)S(1)}, u32[]{:S(2)}, u32[]{:S(2)}) async-start(bf16[8,256,128]{2,1,0:T(8,128)(2,1)} %stack.2), calls=%async_computation | async-start | bytes 1048576 | tf_op jit(solution)/shard_map/all_to_all | solution.py:73
  16.5 240.3 %all-gather.7.cloned.1.call-start = ((), (), s32[]{:S(2)}) async-start(), calls=%async_computation.4 | async-start | bytes 35651584 | tf_op jit(solution)/shard_map/all_gather | solution.py:12
  280.3 64.0 %copy-start.3 = (bf16[256,128]{1,0:T(8,128)(2,1)S(1)}, bf16[256,128]{1,0:T(8,128)(2,1)}, u32[]{:S(2)}) copy-start(bf16[256,128]{1,0:T(8,128)(2,1)} %param.10) | copy-start | bytes 196612
  280.3 64.0 %copy-start.4 = (bf16[128,128]{1,0:T(8,128)(2,1)S(1)}, bf16[128,128]{1,0:T(8,128)(2,1)}, u32[]{:S(2)}) copy-start(bf16[128,128]{1,0:T(8,128)(2,1)} %param.13) | copy-start | bytes 98308
  280.4 82.2 %copy-start.5 = (bf16[128]{0:T(256)(128)(2,1)S(1)}, bf16[128]{0:T(256)(128)(2,1)}, u32[]{:S(2)}) copy-start(bf16[128]{0:T(256)(128)(2,1)} %param.15) | copy-start | bytes 772
  280.4 94.1 %copy-start.2 = (bf16[3,3,128,128]{3,2,1,0:T(8,128)(2,1)S(1)}, bf16[3,3,128,128]{3,2,1,0:T(8,128)(2,1)}, u32[]{:S(2)}) copy-start(bf16[3,3,128,128]{3,2,1,0:T(8,128)(2,1)} %param.14) | copy-start | bytes 884740
  344.2 46.5 %copy-start.1 = (bf16[128,128]{1,0:T(8,128)(2,1)S(1)}, bf16[128,128]{1,0:T(8,128)(2,1)}, u32[]{:S(2)}) copy-start(bf16[128,128]{1,0:T(8,128)(2,1)} %param.12) | copy-start | bytes 98308
  356.1 6.5 %collective-permute-start = (bf16[1,16,128]{2,1,0:T(8,128)(2,1)S(1)}, bf16[1,16,128]{2,1,0:T(8,128)(2,1)S(1)}, u32[]{:S(2)}, u32[]{:S(2)}) collective-permute-start(bf16[1,16,128]{2,1,0:T(8,128)(2,1)S(1)} %copy.19), channel_id=1, source_target_pairs={{0,16},{16,32},{32,48},{48,64},{64,80},{80,96},{96,112},{1,17},{17... | collective-permute-start | bytes 12296 | tf_op jit(solution)/shard_map/ppermute | solution.py:24
  360.6 8.0 %collective-permute-start.1 = (bf16[1,16,128]{2,1,0:T(8,128)(2,1)S(1)}, bf16[1,16,128]{2,1,0:T(8,128)(2,1)S(1)}, u32[]{:S(2)}, u32[]{:S(2)}) collective-permute-start(bf16[1,16,128]{2,1,0:T(8,128)(2,1)S(1)} %copy.20), channel_id=1, source_target_pairs={{16,0},{32,16},{48,32},{64,48},{80,64},{96,80},{112,96},{17,1},{33... | collective-permute-start | bytes 12296 | tf_op jit(solution)/shard_map/ppermute | solution.py:27
  368.6 6.0 %collective-permute-start.2 = (bf16[18,1,128]{2,1,0:T(2,128)(2,1)S(1)}, bf16[18,1,128]{2,1,0:T(2,128)(2,1)S(1)}, u32[]{:S(2)}, u32[]{:S(2)}) collective-permute-start(bf16[18,1,128]{2,1,0:T(2,128)(2,1)S(1)} %get-tuple-element.135), channel_id=1, source_target_pairs={{0,1},{1,2},{2,3},{3,4},{4,5},{5,6},{6,7},{7,8},{8,9},{9,10},{10,1... | collective-permute-start | bytes 13832 | tf_op jit(solution)/shard_map/ppermute | solution.py:24
  372.5 5.0 %collective-permute-start.3 = (bf16[18,1,128]{2,1,0:T(2,128)(2,1)S(1)}, bf16[18,1,128]{2,1,0:T(2,128)(2,1)S(1)}, u32[]{:S(2)}, u32[]{:S(2)}) collective-permute-start(bf16[18,1,128]{2,1,0:T(2,128)(2,1)S(1)} %get-tuple-element.136), channel_id=1, source_target_pairs={{1,0},{2,1},{3,2},{4,3},{5,4},{6,5},{7,6},{8,7},{9,8},{10,9},{11,1... | collective-permute-start | bytes 13832 | tf_op jit(solution)/shard_map/ppermute | solution.py:27
Sparse Core Ops, SparseCore 0:
  9.0 35.2 all-gather.4
  76.1 180.6 all-gather.6
